TPU v7x, 128 devices: a whole 4x4x4 slice. The times are simulated.
128 devices in a mesh: gx: 8 (over y, core), gy: 4 (over z), gz: 4 (over x).
Axes of the slice: x: 4, y: 4, z: 4, core: 2. Of those that a mesh axis runs over, the one named last changes fastest.
Arguments:
- right_side: float32 [128, 64, 1024], P('gx', 'gy', 'gz'), may hold values from -8 to 8
- conductance: float32 [3, 128, 64, 1024], P(None, 'gx', 'gy', 'gz'), may hold values from 0.2 to 5
- storage: float32 [128, 64, 1024], P('gx', 'gy', 'gz'), may hold values from 0.05 to 0.8
- dirichlet: int32 [128, 64, 1024], P('gx', 'gy', 'gz'), may hold values 0 or 1
- basis: float32 [16, 128, 64, 1024], P(None, 'gx', 'gy', 'gz'), may hold values from -2 to 2
- coarse_inverse: float32 [2048, 2048], P(('gx', 'gy', 'gz')), may hold values from 0 to 2, as said below
Outputs:
- solution_field: float32 [128, 64, 1024], P('gx', 'gy', 'gz')
- residual: float32 [128, 64, 1024], P('gx', 'gy', 'gz')
Inputs may be any that keep to these rules, and one draw needn't show every extreme that they name: `coarse_inverse`: symmetric positive definite.
All inputs are finite; a program needn't handle non-finite values. No bound on the sum of `dirichlet` on one device may be relied on, other than what follows from the above.
Results may differ from a plain program's by a relative error of at most 0.0003.
Values sent between devices are 32-bit elements; how exact they have to be, the bound alone decides.
A program may use at most 128 MiB of HBM per device.

v0:
```python
import jax
import jax.numpy as jnp
from jax import lax
from jax.sharding import PartitionSpec as P

SWEEPS = 4
ITERS = 2
RELAX = 2.0 / 3.0


def padded(value, sides, width):
    for axis, dim in sides:
        count, length = (lax.axis_size(axis), value.shape[dim])
        up = [(i, (i + 1) % count) for i in range(count - 1)]
        down = [(j, i) for i, j in up]
        last = lax.slice_in_dim(value, length - width, length, axis=dim)
        leading = lax.slice_in_dim(value, 0, width, axis=dim)
        before = lax.ppermute(last, axis, up)
        after = lax.ppermute(leading, axis, down)
        value = jnp.concatenate([before, value, after], axis=dim)
    return value


def pad_cond(cond):
    return jnp.pad(cond, ((0, 0), (1, 1), (1, 1), (1, 1)))


def stencil(padded_free, padded_cond, field, storage, free):
    middle = padded_free[1:-1, 1:-1, 1:-1]
    total = storage * middle
    total = (
        total
        + padded_cond[0, 1:-1, 1:-1, 1:-1] * (middle - padded_free[2:, 1:-1, 1:-1])
        + padded_cond[0, :-2, 1:-1, 1:-1] * (middle - padded_free[:-2, 1:-1, 1:-1])
    )
    total = (
        total
        + padded_cond[1, 1:-1, 1:-1, 1:-1] * (middle - padded_free[1:-1, 2:, 1:-1])
        + padded_cond[1, 1:-1, :-2, 1:-1] * (middle - padded_free[1:-1, :-2, 1:-1])
    )
    total = (
        total
        + padded_cond[2, 1:-1, 1:-1, 1:-1] * (middle - padded_free[1:-1, 1:-1, 2:])
        + padded_cond[2, 1:-1, 1:-1, :-2] * (middle - padded_free[1:-1, 1:-1, :-2])
    )
    return free * total + (1.0 - free) * field


def diagonal_of(padded_cond, storage, free):
    total = storage + padded_cond[0, 1:-1, 1:-1, 1:-1] + padded_cond[0, :-2, 1:-1, 1:-1]
    total = total + padded_cond[1, 1:-1, 1:-1, 1:-1] + padded_cond[1, 1:-1, :-2, 1:-1]
    total = total + padded_cond[2, 1:-1, 1:-1, 1:-1] + padded_cond[2, 1:-1, 1:-1, :-2]
    return free * total + (1.0 - free)


def jacobi(rhs_box, padded_cond, diagonal, storage_box, free_box):
    guess = jnp.zeros_like(rhs_box)
    for sweep in range(SWEEPS):
        image = stencil(jnp.pad(free_box * guess, 1), padded_cond, guess, storage_box, free_box)
        guess = guess + RELAX * (rhs_box - image) / diagonal
    return guess


def project(basis, field):
    return jnp.dot(
        basis.reshape(basis.shape[0], -1), field.reshape(-1), precision=lax.Precision.HIGHEST
    )


def expand(basis, weights, field):
    return jnp.dot(
        weights, basis.reshape(basis.shape[0], -1), precision=lax.Precision.HIGHEST
    ).reshape(field.shape)


def gather_coarse(values):
    return lax.all_gather(values, ("gx", "gy", "gz"), axis=0, tiled=True)


def residual_rim(field):
    return padded(field, (("gx", 0), ("gy", 1), ("gz", 2)), 2)


def norm_sum(value):
    return lax.psum(value, ("gx", "gy", "gz"))


def shards(right_side, conductance, storage, dirichlet, basis, coarse_inverse):
    free = 1.0 - dirichlet.astype(jnp.float32)
    stacked = jnp.concatenate([conductance, storage[None], free[None]], axis=0)
    wide = padded(stacked, (("gx", 1), ("gy", 2), ("gz", 3)), 3)
    cond_face = wide[:3, 2:-2, 2:-2, 2:-2]
    free_face = wide[4, 2:-2, 2:-2, 2:-2]
    cond_box = wide[:3, 1:-1, 1:-1, 1:-1]
    storage_box = wide[3, 1:-1, 1:-1, 1:-1]
    free_box = wide[4, 1:-1, 1:-1, 1:-1]
    box_cond = pad_cond(cond_box)
    box_diag = diagonal_of(box_cond, storage_box, free_box)

    def schwarz(rhs_box):
        return jacobi(rhs_box, box_cond, box_diag, storage_box, free_box)[2:-2, 2:-2, 2:-2]

    solution = jnp.zeros_like(right_side)
    residual = right_side
    rhs_box = residual_rim(residual)
    coarse_now = project(basis, residual)
    weights = jnp.dot(coarse_inverse, gather_coarse(coarse_now), precision=lax.Precision.HIGHEST)
    precond = schwarz(rhs_box) + expand(basis, weights, residual)
    norm_now = norm_sum(jnp.sum(residual * precond))
    direction = precond
    for step in range(ITERS):
        near_dir = padded(direction, (("gx", 0), ("gy", 1), ("gz", 2)), 1)
        image = stencil(free_face * near_dir, cond_face, direction, storage, free)
        local_curve = jnp.sum(direction * image)
        curvature = lax.psum(local_curve, ("gx", "gy", "gz"))
        alpha = norm_now / curvature
        solution = solution + alpha * direction
        residual = residual - alpha * image
        if step + 1 < ITERS:
            rhs_box = residual_rim(residual)
            coarse_now = project(basis, residual)
            gathered = gather_coarse(coarse_now)
            weights = jnp.dot(coarse_inverse, gathered, precision=lax.Precision.HIGHEST)
            precond = schwarz(rhs_box) + expand(basis, weights, residual)
            norm_next = norm_sum(jnp.sum(residual * precond))
            direction = precond + norm_next / norm_now * direction
            norm_now = norm_next
    return (solution, residual)


def solution(mesh):
    placed = (
        P("gx", "gy", "gz"),
        P(None, "gx", "gy", "gz"),
        P("gx", "gy", "gz"),
        P("gx", "gy", "gz"),
        P(None, "gx", "gy", "gz"),
        P(("gx", "gy", "gz"), None),
    )
    return jax.shard_map(
        shards,
        mesh=mesh,
        in_specs=placed,
        out_specs=(P("gx", "gy", "gz"), P("gx", "gy", "gz")),
        check_vma=False,
    )
```

profile of v0, /device:TPU:1, one launch (start us, length us, event | category | flops | bytes accessed | tf_op | source)
XLA Modules:
  0.0 572.3 jit_solution(1241836847515531308)
XLA Ops:
  2.9 4.6 collective-permute-start.6
  10.3 3.6 collective-permute-start
  15.8 8.8 %fusion.8 = f32[16]{0:T(128)S(1)} fusion(f32[16,16,16,256]{3,2,1,0:T(8,128)} %param.10, f32[16,16,256,1]{2,1,0,3:T(8,128)} %bitcast.289), kind=kOutput, calls=%fused_computation.14 | convolution fusion | flops 12582912 | bytes 4456512 | tf_op jit(solution)/shard_map/dot_general | solution.py:65
  24.8 66.8 %all-reduce.8 = f32[2048]{0:T(1024)S(1)} all-reduce(f32[2048]{0:T(1024)S(1)} %dynamic-update-slice), channel_id=1, replica_groups=mesh['gx'=8,'gy'=4,'gz'=4] {'gx','gy','gz'}, use_global_device_ids=true, to_apply=%add.8 | all-reduce | flops 2048 | bytes 16384
  98.7 4.7 collective-permute-start.8
  105.7 5.1 fusion.2
  110.9 8.1 %copy.37 = f32[5,22,16,256]{2,1,3,0:T(8,128)} copy(f32[5,22,16,256]{3,2,1,0:T(8,128)S(1)} %pad_maximum_fusion.2) | data formatting | bytes 3604480 | tf_op jit(solution)/shard_map/concatenate | solution.py:20
  119.0 9.0 %copy.36 = f32[5,22,3,256]{2,1,3,0:T(8,128)} copy(f32[5,22,3,256]{3,1,2,0:T(8,128)} %collective-permute-done.8) | data formatting | bytes 675840 | tf_op jit(solution)/shard_map/ppermute | solution.py:18
  128.0 9.0 %copy.38 = f32[5,22,3,256]{2,1,3,0:T(8,128)} copy(f32[5,22,3,256]{3,1,2,0:T(8,128)} %collective-permute-done.9) | data formatting | bytes 675840 | tf_op jit(solution)/shard_map/ppermute | solution.py:19
  137.0 16.9 %pad_maximum_fusion = f32[5,22,22,256]{2,1,3,0:T(8,128)S(1)} fusion(f32[5,22,3,256]{2,1,3,0:T(8,128)} %copy.38, f32[5,22,16,256]{2,1,3,0:T(8,128)} %copy.37, f32[5,22,3,256]{2,1,3,0:T(8,128)} %copy.36), kind=kLoop, calls=%fused_computation | loop fusion | flops 1239040 | bytes 4956160 | tf_op jit(solution)/shard_map/concatenate | solution.py:20
  153.8 5.4 copy-done.4
  164.9 4.0 collective-permute-start.4
  170.4 9.2 %copy.40 = f32[5,22,22,256]{3,2,1,0:T(8,128)S(1)} copy(f32[5,22,22,256]{2,1,3,0:T(8,128)} %copy-done.4) | data formatting | bytes 4956160 | tf_op jit(solution)/shard_map/concatenate | solution.py:20
  179.6 3.1 copy.39
  184.6 3.2 pad_maximum_fusion.1
  191.2 3.7 fusion.213
  203.7 4.9 collective-permute-start.12
  213.7 4.3 collective-permute-start.14
  219.3 3.2 collective-permute-done.15
  222.7 4.3 collective-permute-start.16
  232.2 3.9 collective-permute-done.17
  239.0 63.0 %all-reduce.10 = (f32[]{:T(128)}, f32[]{:T(128)}) all-reduce(f32[]{:T(128)} %get-tuple-element.5, f32[]{:T(128)} %get-tuple-element.4), channel_id=1, replica_groups=mesh['gx'=8,'gy'=4,'gz'=4] {'gx','gy','gz'}, use_global_device_ids=true, to_apply=%region_1.2 | all-reduce | flops 2 | bytes 16 | tf_op jit(solution)/shard_map/psum | solution.py:85
  304.5 3.0 collective-permute-start.18
  309.4 8.6 %fusion.11 = f32[16]{0:T(128)S(1)} fusion(f32[16,16,16,256]{3,2,1,0:T(8,128)} %param.10, f32[16,16,256,1]{2,1,0,3:T(8,128)S(1)} %bitcast.285), kind=kOutput, calls=%fused_computation.15 | convolution fusion | flops 12582912 | bytes 4456512 | tf_op jit(solution)/shard_map/dot_general | solution.py:65
  318.3 63.0 %all-reduce.9 = f32[2048]{0:T(1024)S(1)} all-reduce(f32[2048]{0:T(1024)S(1)} %dynamic-update-slice.1), channel_id=1, replica_groups=mesh['gx'=8,'gy'=4,'gz'=4] {'gx','gy','gz'}, use_global_device_ids=true, to_apply=%add.9 | all-reduce | flops 2048 | bytes 16384
  385.6 3.2 collective-permute-done.21
  392.3 6.4 %fusion = f32[1,16,16,256]{3,0,2,1:T(1,128)S(1)} fusion(f32[16,1,1,1]{0,1,3,2:T(1,128)S(1)} %convolution_bitcast_fusion, f32[16,16,256,16]{2,1,0,3:T(8,128)} %bitcast.283), kind=kOutput, calls=%fused_computation.2 | convolution fusion | flops 12582912 | bytes 4456512 | tf_op jit(solution)/shard_map/dot_general | solution.py:71
  407.6 67.1 %psum.30 = f32[]{:T(128)} all-reduce(f32[]{:T(128)} %get-tuple-element.10), channel_id=1, replica_groups=mesh['gx'=8,'gy'=4,'gz'=4] {'gx','gy','gz'}, use_global_device_ids=true, to_apply=%region_5.6 | all-reduce | flops 1 | bytes 8 | tf_op jit(solution)/shard_map/psum | solution.py:85
  488.0 3.2 collective-permute-done.27
  494.6 3.9 collective-permute-done.28
  498.5 3.9 collective-permute-done.29
  506.7 63.2 %psum.31 = f32[]{:T(128)} all-reduce(f32[]{:T(128)} %get-tuple-element.8), channel_id=1, replica_groups=mesh['gx'=8,'gy'=4,'gz'=4] {'gx','gy','gz'}, use_global_device_ids=true, to_apply=%region_7.8 | all-reduce | flops 1 | bytes 8 | tf_op jit(solution)/shard_map/psum | solution.py:115
  (162 shorter events, 92.3 us)
Async XLA Ops:
  1.8 95.9 %copy-start.18 = (f32[1,16,16,256]{3,2,1,0:T(8,128)}, f32[1,16,16,256]{3,2,1,0:T(8,128)S(1)}, u32[]{:S(2)}) copy-start(f32[1,16,16,256]{3,2,1,0:T(8,128)S(1)} %fusion.212) | copy-start | bytes 786436
  2.9 92.8 %collective-permute-start.6 = (f32[5,3,16,256]{3,2,1,0:T(8,128)S(1)}, f32[5,3,16,256]{3,2,1,0:T(8,128)S(1)}, u32[]{:S(2)}, u32[]{:S(2)}) collective-permute-start(f32[5,3,16,256]{3,2,1,0:T(8,128)S(1)} %get-tuple-element.36), channel_id=1, source_target_pairs={{0,16},{16,32},{32,48},{48,64},{64,80},{80,96},{96,112},{1,17},{17... | collective-permute-start | bytes 737288 | tf_op jit(solution)/shard_map/ppermute | solution.py:18
  7.6 88.9 %collective-permute-start.7 = (f32[5,3,16,256]{3,2,1,0:T(8,128)S(1)}, f32[5,3,16,256]{3,2,1,0:T(8,128)}, u32[]{:S(2)}, u32[]{:S(2)}) collective-permute-start(f32[5,3,16,256]{3,2,1,0:T(8,128)S(1)} %get-tuple-element.37), channel_id=1, source_target_pairs={{16,0},{32,16},{48,32},{64,48},{80,64},{96,80},{112,96},{17,1},{33... | collective-permute-start | bytes 737288 | tf_op jit(solution)/shard_map/ppermute | solution.py:19
  10.3 81.6 %collective-permute-start = (f32[2,16,256]{2,1,0:T(8,128)S(1)}, f32[2,16,256]{2,1,0:T(8,128)S(1)}, u32[]{:S(2)}, u32[]{:S(2)}) collective-permute-start(f32[2,16,256]{2,1,0:T(8,128)S(1)} %get-tuple-element.61), channel_id=1, source_target_pairs={{0,16},{16,32},{32,48},{48,64},{64,80},{80,96},{96,112},{1,17},{17... | collective-permute-start | bytes 98312 | tf_op jit(solution)/shard_map/ppermute | solution.py:18
  13.9 78.1 %collective-permute-start.1 = (f32[2,16,256]{2,1,0:T(8,128)S(1)}, f32[2,16,256]{2,1,0:T(8,128)S(1)}, u32[]{:S(2)}, u32[]{:S(2)}) collective-permute-start(f32[2,16,256]{2,1,0:T(8,128)S(1)} %get-tuple-element.60), channel_id=1, source_target_pairs={{16,0},{32,16},{48,32},{64,48},{80,64},{96,80},{112,96},{17,1},{33... | collective-permute-start | bytes 98312 | tf_op jit(solution)/shard_map/ppermute | solution.py:19
  92.0 18.7 %collective-permute-start.2 = (f32[20,2,256]{2,1,0:T(2,128)S(1)}, f32[20,2,256]{2,1,0:T(2,128)S(1)}, u32[]{:S(2)}, u32[]{:S(2)}) collective-permute-start(f32[20,2,256]{2,1,0:T(2,128)S(1)} %get-tuple-element.48), channel_id=1, source_target_pairs={{0,4},{4,8},{8,12},{1,5},{5,9},{9,13},{2,6},{6,10},{10,14},{3,7},{... | collective-permute-start | bytes 122888 | tf_op jit(solution)/shard_map/ppermute | solution.py:18
  94.5 16.3 %collective-permute-start.3 = (f32[20,2,256]{2,1,0:T(2,128)S(1)}, f32[20,2,256]{2,1,0:T(2,128)S(1)}, u32[]{:S(2)}, u32[]{:S(2)}) collective-permute-start(f32[20,2,256]{2,1,0:T(2,128)S(1)} %get-tuple-element.49), channel_id=1, source_target_pairs={{4,0},{8,4},{12,8},{5,1},{9,5},{13,9},{6,2},{10,6},{14,10},{7,3},{... | collective-permute-start | bytes 122888 | tf_op jit(solution)/shard_map/ppermute | solution.py:19
  98.7 20.3 %collective-permute-start.8 = (f32[5,22,3,256]{3,1,2,0:T(8,128)}, f32[5,22,3,256]{3,1,2,0:T(8,128)}, u32[]{:S(2)}, u32[]{:S(2)}) collective-permute-start(f32[5,22,3,256]{3,1,2,0:T(8,128)} %copy.55), channel_id=1, source_target_pairs={{0,4},{4,8},{8,12},{1,5},{5,9},{9,13},{2,6},{6,10},{10,14},{3,7},{... | collective-permute-start | bytes 1013768 | tf_op jit(solution)/shard_map/ppermute | solution.py:18
  104.3 23.8 %collective-permute-start.9 = (f32[5,22,3,256]{3,1,2,0:T(8,128)}, f32[5,22,3,256]{3,1,2,0:T(8,128)}, u32[]{:S(2)}, u32[]{:S(2)}) collective-permute-start(f32[5,22,3,256]{3,1,2,0:T(8,128)} %copy.56), channel_id=1, source_target_pairs={{4,0},{8,4},{12,8},{5,1},{9,5},{13,9},{6,2},{10,6},{14,10},{7,3},{... | collective-permute-start | bytes 1013768 | tf_op jit(solution)/shard_map/ppermute | solution.py:19
  160.0 19.6 %collective-permute-start.10 = (f32[5,22,22,3]{2,1,3,0:T(8,128)}, f32[5,22,22,3]{2,1,3,0:T(8,128)}, u32[]{:S(2)}, u32[]{:S(2)}) collective-permute-start(f32[5,22,22,3]{2,1,3,0:T(8,128)} %get-tuple-element.30), channel_id=1, source_target_pairs={{0,1},{1,2},{2,3},{4,5},{5,6},{6,7},{8,9},{9,10},{10,11},{12,13},{... | collective-permute-start | bytes 87128 | tf_op jit(solution)/shard_map/ppermute | solution.py:18
  162.7 20.0 %collective-permute-start.11 = (f32[5,22,22,3]{2,1,3,0:T(8,128)}, f32[5,22,22,3]{2,1,3,0:T(8,128)S(1)}, u32[]{:S(2)}, u32[]{:S(2)}) collective-permute-start(f32[5,22,22,3]{2,1,3,0:T(8,128)} %get-tuple-element.31), channel_id=1, source_target_pairs={{1,0},{2,1},{3,2},{5,4},{6,5},{7,6},{9,8},{10,9},{11,10},{13,12},{... | collective-permute-start | bytes 87128 | tf_op jit(solution)/shard_map/ppermute | solution.py:19
  164.9 25.7 %collective-permute-start.4 = (f32[20,20,2]{2,1,0:T(8,128)}, f32[20,20,2]{2,1,0:T(8,128)S(1)}, u32[]{:S(2)}, u32[]{:S(2)}) collective-permute-start(f32[20,20,2]{2,1,0:T(8,128)} %get-tuple-element.40), channel_id=1, source_target_pairs={{0,1},{1,2},{2,3},{4,5},{5,6},{6,7},{8,9},{9,10},{10,11},{12,13},{... | collective-permute-start | bytes 9608 | tf_op jit(solution)/shard_map/ppermute | solution.py:18
  168.9 22.4 %collective-permute-start.5 = (f32[20,20,2]{2,1,0:T(8,128)}, f32[20,20,2]{2,1,0:T(8,128)}, u32[]{:S(2)}, u32[]{:S(2)}) collective-permute-start(f32[20,20,2]{2,1,0:T(8,128)} %get-tuple-element.41), channel_id=1, source_target_pairs={{1,0},{2,1},{3,2},{5,4},{6,5},{7,6},{9,8},{10,9},{11,10},{13,12},{... | collective-permute-start | bytes 9608 | tf_op jit(solution)/shard_map/ppermute | solution.py:19
  203.7 7.3 %collective-permute-start.12 = (f32[1,16,256]{2,1,0:T(8,128)S(1)}, f32[1,16,256]{2,1,0:T(8,128)S(1)}, u32[]{:S(2)}, u32[]{:S(2)}) collective-permute-start(f32[1,16,256]{2,1,0:T(8,128)S(1)} %get-tuple-element.58), channel_id=1, source_target_pairs={{0,16},{16,32},{32,48},{48,64},{64,80},{80,96},{96,112},{1,17},{17... | collective-permute-start | bytes 49160 | tf_op jit(solution)/shard_map/ppermute | solution.py:18
  208.6 5.1 collective-permute-start.13
  213.7 5.6 collective-permute-start.14
  218.0 4.5 collective-permute-start.15
  222.7 9.5 %collective-permute-start.16 = (f32[18,18,1]{2,1,0:T(8,128)S(1)}, f32[18,18,1]{2,1,0:T(8,128)S(1)}, u32[]{:S(2)}, u32[]{:S(2)}) collective-permute-start(f32[18,18,1]{2,1,0:T(8,128)S(1)} %get-tuple-element.44), channel_id=1, source_target_pairs={{0,1},{1,2},{2,3},{4,5},{5,6},{6,7},{8,9},{9,10},{10,11},{12,13},{... | collective-permute-start | bytes 3896 | tf_op jit(solution)/shard_map/ppermute | solution.py:18
  227.0 9.1 %collective-permute-start.17 = (f32[18,18,1]{2,1,0:T(8,128)S(1)}, f32[18,18,1]{2,1,0:T(8,128)S(1)}, u32[]{:S(2)}, u32[]{:S(2)}) collective-permute-start(f32[18,18,1]{2,1,0:T(8,128)S(1)} %get-tuple-element.45), channel_id=1, source_target_pairs={{1,0},{2,1},{3,2},{5,4},{6,5},{7,6},{9,8},{10,9},{11,10},{13,12},{... | collective-permute-start | bytes 3896 | tf_op jit(solution)/shard_map/ppermute | solution.py:19
  304.5 76.9 %collective-permute-start.18 = (f32[2,16,256]{2,1,0:T(8,128)S(1)}, f32[2,16,256]{2,1,0:T(8,128)S(1)}, u32[]{:S(2)}, u32[]{:S(2)}) collective-permute-start(f32[2,16,256]{2,1,0:T(8,128)S(1)} %get-tuple-element.56), channel_id=1, source_target_pairs={{0,16},{16,32},{32,48},{48,64},{64,80},{80,96},{96,112},{1,17},{17... | collective-permute-start | bytes 98312 | tf_op jit(solution)/shard_map/ppermute | solution.py:18
  307.5 73.8 %collective-permute-start.19 = (f32[2,16,256]{2,1,0:T(8,128)S(1)}, f32[2,16,256]{2,1,0:T(8,128)S(1)}, u32[]{:S(2)}, u32[]{:S(2)}) collective-permute-start(f32[2,16,256]{2,1,0:T(8,128)S(1)} %get-tuple-element.57), channel_id=1, source_target_pairs={{16,0},{32,16},{48,32},{64,48},{80,64},{96,80},{112,96},{17,1},{33... | collective-permute-start | bytes 98312 | tf_op jit(solution)/shard_map/ppermute | solution.py:19
  381.4 4.2 collective-permute-start.20
  384.1 4.7 collective-permute-start.21
  389.0 9.7 %collective-permute-start.22 = (f32[20,20,2]{2,1,0:T(8,128)S(1)}, f32[20,20,2]{2,1,0:T(8,128)S(1)}, u32[]{:S(2)}, u32[]{:S(2)}) collective-permute-start(f32[20,20,2]{2,1,0:T(8,128)S(1)} %get-tuple-element.38), channel_id=1, source_target_pairs={{0,1},{1,2},{2,3},{4,5},{5,6},{6,7},{8,9},{9,10},{10,11},{12,13},{... | collective-permute-start | bytes 9608 | tf_op jit(solution)/shard_map/ppermute | solution.py:18
  390.8 7.9 %collective-permute-start.23 = (f32[20,20,2]{2,1,0:T(8,128)S(1)}, f32[20,20,2]{2,1,0:T(8,128)S(1)}, u32[]{:S(2)}, u32[]{:S(2)}) collective-permute-start(f32[20,20,2]{2,1,0:T(8,128)S(1)} %get-tuple-element.39), channel_id=1, source_target_pairs={{1,0},{2,1},{3,2},{5,4},{6,5},{7,6},{9,8},{10,9},{11,10},{13,12},{... | collective-permute-start | bytes 9608 | tf_op jit(solution)/shard_map/ppermute | solution.py:19
  405.0 99.2 %copy-start.9 = (f32[3,16,16,256]{3,2,1,0:T(8,128)S(1)}, f32[3,16,16,256]{3,2,1,0:T(8,128)}, u32[]{:S(2)}) copy-start(f32[3,16,16,256]{3,2,1,0:T(8,128)} %param.7) | copy-start | bytes 2359300
  476.9 4.3 collective-permute-start.24
  479.1 5.1 collective-permute-start.25
  484.2 3.8 collective-permute-start.26
  486.6 4.6 collective-permute-start.27
  491.4 7.1 %collective-permute-start.28 = (f32[18,18,1]{2,1,0:T(8,128)S(1)}, f32[18,18,1]{2,1,0:T(8,128)S(1)}, u32[]{:S(2)}, u32[]{:S(2)}) collective-permute-start(f32[18,18,1]{2,1,0:T(8,128)S(1)} %get-tuple-element.42), channel_id=1, source_target_pairs={{0,1},{1,2},{2,3},{4,5},{5,6},{6,7},{8,9},{9,10},{10,11},{12,13},{... | collective-permute-start | bytes 3896 | tf_op jit(solution)/shard_map/ppermute | solution.py:18
  493.3 9.1 %collective-permute-start.29 = (f32[18,18,1]{2,1,0:T(8,128)S(1)}, f32[18,18,1]{2,1,0:T(8,128)S(1)}, u32[]{:S(2)}, u32[]{:S(2)}) collective-permute-start(f32[18,18,1]{2,1,0:T(8,128)S(1)} %get-tuple-element.43), channel_id=1, source_target_pairs={{1,0},{2,1},{3,2},{5,4},{6,5},{7,6},{9,8},{10,9},{11,10},{13,12},{... | collective-permute-start | bytes 3896 | tf_op jit(solution)/shard_map/ppermute | solution.py:19
  (30 other events, 940.6 us)
where the time goes:
time: 581 us; the launch traced here: 572 us
  blocking collectives  323 us (56%)
  starting transfers between devices  73.3 us (13%)
  local copies, waits for them, and re-layouts  55.9 us (10%)
  other arithmetic  55.2 us (10%)
  waiting for transfers between devices  29.9 us (5%)
  matrix products  29.2 us (5%)
    psum x2, blocking collectives, norm_sum(): return lax.psum(value, ('gx', 'gy', 'gz'))  130 us
    unnamed x2, blocking collectives  130 us
    psum x1, blocking collectives, shards(): curvature = lax.psum(local_curve, ('gx', 'gy', 'gz'))  63.2 us
    ppermute x15, starting transfers between devices, padded(): before = lax.ppermute(last, axis, up)  49.5 us
    ppermute x15, starting transfers between devices, padded(): after = lax.ppermute(leading, axis, down)  23.7 us
    ppermute x15, waiting for transfers between devices, padded(): after = lax.ppermute(leading, axis, down)  23.2 us
    concatenate x7, other arithmetic, padded(): value = jnp.concatenate([before, value, after], axis=dim)  21.5 us
    dot_general x2, matrix products, project(): jnp.dot(basis.reshape(basis.shape[0], -1), field.reshape(-1), precision=l...  17.4 us
  transfers between devices with their start and end apart: 30, of which 9 were waited for; matrix products, arithmetic and copies ran while one was open for 13% of the time, Pallas kernels for 0%

commit v1 on v0

--- a/solution.py
+++ b/solution.py
@@ -82,7 +82,10 @@
 
 
 def norm_sum(value):
-    return lax.psum(value, ("gx", "gy", "gz"))
+    cards_proceed = lambda chunk, dev_axis, along_axis: lax.psum(
+        lax.psum(chunk, dev_axis), along_axis
+    )
+    return cards_proceed(value, ("gy", "gz"), "gx")
 
 
 def shards(right_side, conductance, storage, dirichlet, basis, coarse_inverse):

time: 581 us -> 615 us (1.059)
  blocking collectives: 323 us -> 359 us
    psum x1 -> x2, blocking collectives: 63.2 us -> 124 us  [shards(): curvature = lax.psum(local_curve, ('gx', 'gy', 'gz'))]
    psum x2 -> x4, blocking collectives: 130 us -> 105 us  [the longest x2 63 us: norm_sum(): lax.psum(chunk, dev_axis)]
  transfers between devices with their start and end apart: 30 -> 30, of which waited for: 9 -> 9; matrix products, arithmetic and copies ran while one was open for 13% -> 12% of each run, Pallas kernels for 0% -> 0%
where the time goes in v1:
time: 615 us; the launch traced here: 607 us
  blocking collectives  359 us (58%)
  starting transfers between devices  72.1 us (12%)
  local copies, waits for them, and re-layouts  56.2 us (9%)
  other arithmetic  55.1 us (9%)
  waiting for transfers between devices  29.4 us (5%)
  matrix products  29.2 us (5%)
    unnamed x2, blocking collectives  130 us
    psum x2, blocking collectives, shards(): curvature = lax.psum(local_curve, ('gx', 'gy', 'gz'))  124 us
    psum x2, blocking collectives, norm_sum(): lax.psum(chunk, dev_axis)  63 us
    ppermute x15, starting transfers between devices, padded(): before = lax.ppermute(last, axis, up)  47.8 us
    psum x2, blocking collectives, norm_sum(): lax.psum(lax.psum(chunk, dev_axis), along_axis)  41.7 us
    ppermute x15, starting transfers between devices, padded(): after = lax.ppermute(leading, axis, down)  24.3 us
    ppermute x15, waiting for transfers between devices, padded(): after = lax.ppermute(leading, axis, down)  23 us
    concatenate x7, other arithmetic, padded(): value = jnp.concatenate([before, value, after], axis=dim)  21.5 us
  transfers between devices with their start and end apart: 30, of which 9 were waited for; matrix products, arithmetic and copies ran while one was open for 12% of the time, Pallas kernels for 0%

profile of v1, /device:TPU:1, one launch (start us, length us, event | category | flops | bytes accessed | tf_op | source)
XLA Modules:
  0.0 606.7 jit_solution(3490721301809254384)
XLA Ops:
  2.9 4.6 collective-permute-start.6
  10.3 3.6 collective-permute-start
  15.8 8.8 %fusion.8 = f32[16]{0:T(128)S(1)} fusion(f32[16,16,16,256]{3,2,1,0:T(8,128)} %param.10, f32[16,16,256,1]{2,1,0,3:T(8,128)} %bitcast.289), kind=kOutput, calls=%fused_computation.14 | convolution fusion | flops 12582912 | bytes 4456512 | tf_op jit(solution)/shard_map/dot_general | solution.py:65
  24.8 66.8 %all-reduce.8 = f32[2048]{0:T(1024)S(1)} all-reduce(f32[2048]{0:T(1024)S(1)} %dynamic-update-slice), channel_id=1, replica_groups=mesh['gx'=8,'gy'=4,'gz'=4] {'gx','gy','gz'}, use_global_device_ids=true, to_apply=%add.8 | all-reduce | flops 2048 | bytes 16384
  98.7 4.7 collective-permute-start.8
  105.7 5.1 fusion.2
  110.9 8.1 %copy.37 = f32[5,22,16,256]{2,1,3,0:T(8,128)} copy(f32[5,22,16,256]{3,2,1,0:T(8,128)S(1)} %pad_maximum_fusion.2) | data formatting | bytes 3604480 | tf_op jit(solution)/shard_map/concatenate | solution.py:20
  119.0 9.1 %copy.36 = f32[5,22,3,256]{2,1,3,0:T(8,128)} copy(f32[5,22,3,256]{3,1,2,0:T(8,128)} %collective-permute-done.8) | data formatting | bytes 675840 | tf_op jit(solution)/shard_map/ppermute | solution.py:18
  128.2 9.0 %copy.38 = f32[5,22,3,256]{2,1,3,0:T(8,128)} copy(f32[5,22,3,256]{3,1,2,0:T(8,128)} %collective-permute-done.9) | data formatting | bytes 675840 | tf_op jit(solution)/shard_map/ppermute | solution.py:19
  137.2 16.9 %pad_maximum_fusion = f32[5,22,22,256]{2,1,3,0:T(8,128)S(1)} fusion(f32[5,22,3,256]{2,1,3,0:T(8,128)} %copy.38, f32[5,22,16,256]{2,1,3,0:T(8,128)} %copy.37, f32[5,22,3,256]{2,1,3,0:T(8,128)} %copy.36), kind=kLoop, calls=%fused_computation | loop fusion | flops 1239040 | bytes 4956160 | tf_op jit(solution)/shard_map/concatenate | solution.py:20
  154.0 5.4 copy-done.4
  165.1 4.0 collective-permute-start.4
  170.6 9.2 %copy.40 = f32[5,22,22,256]{3,2,1,0:T(8,128)S(1)} copy(f32[5,22,22,256]{2,1,3,0:T(8,128)} %copy-done.4) | data formatting | bytes 4956160 | tf_op jit(solution)/shard_map/concatenate | solution.py:20
  191.5 3.7 fusion.213
  204.0 4.9 collective-permute-start.12
  214.0 4.3 collective-permute-start.14
  219.6 3.2 collective-permute-done.15
  223.0 4.3 collective-permute-start.16
  232.5 3.9 collective-permute-done.17
  239.3 29.8 %psum.42 = f32[]{:T(128)} all-reduce(f32[]{:T(128)} %get-tuple-element.5), channel_id=1, replica_groups=mesh['gx'=8,'gy'=4,'gz'=4] {'gy','gz'}, use_global_device_ids=true, to_apply=%region_1.2 | all-reduce | flops 1 | bytes 8 | tf_op jit(solution)/shard_map/psum | solution.py:86
  269.1 20.0 %psum.43 = f32[]{:T(128)} all-reduce(f32[]{:T(128)} %psum.42), channel_id=1, replica_groups=mesh['gx'=8,'gy'=4,'gz'=4] {'gx'}, use_global_device_ids=true, to_apply=%region_2.3 | all-reduce | flops 1 | bytes 8 | tf_op jit(solution)/shard_map/psum | solution.py:85
  289.1 62.4 %psum.44 = f32[]{:T(128)} all-reduce(f32[]{:T(128)} %get-tuple-element.4), channel_id=1, replica_groups=mesh['gx'=8,'gy'=4,'gz'=4] {'gx','gy','gz'}, use_global_device_ids=true, to_apply=%region_4.5 | all-reduce | flops 1 | bytes 8 | tf_op jit(solution)/shard_map/psum | solution.py:118
  353.9 3.3 collective-permute-start.18
  359.2 8.6 %fusion.11 = f32[16]{0:T(128)S(1)} fusion(f32[16,16,16,256]{3,2,1,0:T(8,128)} %param.10, f32[16,16,256,1]{2,1,0,3:T(8,128)S(1)} %bitcast.285), kind=kOutput, calls=%fused_computation.15 | convolution fusion | flops 12582912 | bytes 4456512 | tf_op jit(solution)/shard_map/dot_general | solution.py:65
  368.0 63.1 %all-reduce.9 = f32[2048]{0:T(1024)S(1)} all-reduce(f32[2048]{0:T(1024)S(1)} %dynamic-update-slice.1), channel_id=1, replica_groups=mesh['gx'=8,'gy'=4,'gz'=4] {'gx','gy','gz'}, use_global_device_ids=true, to_apply=%add.9 | all-reduce | flops 2048 | bytes 16384
  435.2 3.2 collective-permute-done.21
  442.1 6.4 %fusion = f32[1,16,16,256]{3,0,2,1:T(1,128)S(1)} fusion(f32[16,1,1,1]{0,1,3,2:T(1,128)S(1)} %convolution_bitcast_fusion, f32[16,16,256,16]{2,1,0,3:T(8,128)} %bitcast.283), kind=kOutput, calls=%fused_computation.2 | convolution fusion | flops 12582912 | bytes 4456512 | tf_op jit(solution)/shard_map/dot_general | solution.py:71
  457.4 33.2 %psum.45 = f32[]{:T(128)} all-reduce(f32[]{:T(128)} %get-tuple-element.8), channel_id=1, replica_groups=mesh['gx'=8,'gy'=4,'gz'=4] {'gy','gz'}, use_global_device_ids=true, to_apply=%region_6.7 | all-reduce | flops 1 | bytes 8 | tf_op jit(solution)/shard_map/psum | solution.py:86
  490.6 21.6 %psum.46 = f32[]{:T(128)} all-reduce(f32[]{:T(128)} %psum.45), channel_id=1, replica_groups=mesh['gx'=8,'gy'=4,'gz'=4] {'gx'}, use_global_device_ids=true, to_apply=%region_7.8 | all-reduce | flops 1 | bytes 8 | tf_op jit(solution)/shard_map/psum | solution.py:85
  530.5 3.6 collective-permute-done.28
  534.1 4.1 collective-permute-done.29
  542.4 61.9 %psum.47 = f32[]{:T(128)} all-reduce(f32[]{:T(128)} %get-tuple-element.6), channel_id=1, replica_groups=mesh['gx'=8,'gy'=4,'gz'=4] {'gx','gy','gz'}, use_global_device_ids=true, to_apply=%region_9.10 | all-reduce | flops 1 | bytes 8 | tf_op jit(solution)/shard_map/psum | solution.py:118
  (165 shorter events, 100.0 us)
Async XLA Ops:
  0.6 95.9 %copy-start.15 = (f32[16,16,256]{2,1,0:T(8,128)S(1)}, f32[16,16,256]{2,1,0:T(8,128)}, u32[]{:S(2)}) copy-start(f32[16,16,256]{2,1,0:T(8,128)} %param.8) | copy-start | bytes 786436
  1.8 96.0 %copy-start.18 = (f32[1,16,16,256]{3,2,1,0:T(8,128)}, f32[1,16,16,256]{3,2,1,0:T(8,128)S(1)}, u32[]{:S(2)}) copy-start(f32[1,16,16,256]{3,2,1,0:T(8,128)S(1)} %fusion.212) | copy-start | bytes 786436
  2.9 92.8 %collective-permute-start.6 = (f32[5,3,16,256]{3,2,1,0:T(8,128)S(1)}, f32[5,3,16,256]{3,2,1,0:T(8,128)S(1)}, u32[]{:S(2)}, u32[]{:S(2)}) collective-permute-start(f32[5,3,16,256]{3,2,1,0:T(8,128)S(1)} %get-tuple-element.34), channel_id=1, source_target_pairs={{0,16},{16,32},{32,48},{48,64},{64,80},{80,96},{96,112},{1,17},{17... | collective-permute-start | bytes 737288 | tf_op jit(solution)/shard_map/ppermute | solution.py:18
  7.6 88.9 %collective-permute-start.7 = (f32[5,3,16,256]{3,2,1,0:T(8,128)S(1)}, f32[5,3,16,256]{3,2,1,0:T(8,128)}, u32[]{:S(2)}, u32[]{:S(2)}) collective-permute-start(f32[5,3,16,256]{3,2,1,0:T(8,128)S(1)} %get-tuple-element.35), channel_id=1, source_target_pairs={{16,0},{32,16},{48,32},{64,48},{80,64},{96,80},{112,96},{17,1},{33... | collective-permute-start | bytes 737288 | tf_op jit(solution)/shard_map/ppermute | solution.py:19
  10.3 81.6 %collective-permute-start = (f32[2,16,256]{2,1,0:T(8,128)S(1)}, f32[2,16,256]{2,1,0:T(8,128)S(1)}, u32[]{:S(2)}, u32[]{:S(2)}) collective-permute-start(f32[2,16,256]{2,1,0:T(8,128)S(1)} %get-tuple-element.59), channel_id=1, source_target_pairs={{0,16},{16,32},{32,48},{48,64},{64,80},{80,96},{96,112},{1,17},{17... | collective-permute-start | bytes 98312 | tf_op jit(solution)/shard_map/ppermute | solution.py:18
  13.9 78.1 %collective-permute-start.1 = (f32[2,16,256]{2,1,0:T(8,128)S(1)}, f32[2,16,256]{2,1,0:T(8,128)S(1)}, u32[]{:S(2)}, u32[]{:S(2)}) collective-permute-start(f32[2,16,256]{2,1,0:T(8,128)S(1)} %get-tuple-element.58), channel_id=1, source_target_pairs={{16,0},{32,16},{48,32},{64,48},{80,64},{96,80},{112,96},{17,1},{33... | collective-permute-start | bytes 98312 | tf_op jit(solution)/shard_map/ppermute | solution.py:19
  92.0 18.7 %collective-permute-start.2 = (f32[20,2,256]{2,1,0:T(2,128)S(1)}, f32[20,2,256]{2,1,0:T(2,128)S(1)}, u32[]{:S(2)}, u32[]{:S(2)}) collective-permute-start(f32[20,2,256]{2,1,0:T(2,128)S(1)} %get-tuple-element.46), channel_id=1, source_target_pairs={{0,4},{4,8},{8,12},{1,5},{5,9},{9,13},{2,6},{6,10},{10,14},{3,7},{... | collective-permute-start | bytes 122888 | tf_op jit(solution)/shard_map/ppermute | solution.py:18
  94.5 16.3 %collective-permute-start.3 = (f32[20,2,256]{2,1,0:T(2,128)S(1)}, f32[20,2,256]{2,1,0:T(2,128)S(1)}, u32[]{:S(2)}, u32[]{:S(2)}) collective-permute-start(f32[20,2,256]{2,1,0:T(2,128)S(1)} %get-tuple-element.47), channel_id=1, source_target_pairs={{4,0},{8,4},{12,8},{5,1},{9,5},{13,9},{6,2},{10,6},{14,10},{7,3},{... | collective-permute-start | bytes 122888 | tf_op jit(solution)/shard_map/ppermute | solution.py:19
  98.7 20.3 %collective-permute-start.8 = (f32[5,22,3,256]{3,1,2,0:T(8,128)}, f32[5,22,3,256]{3,1,2,0:T(8,128)}, u32[]{:S(2)}, u32[]{:S(2)}) collective-permute-start(f32[5,22,3,256]{3,1,2,0:T(8,128)} %copy.55), channel_id=1, source_target_pairs={{0,4},{4,8},{8,12},{1,5},{5,9},{9,13},{2,6},{6,10},{10,14},{3,7},{... | collective-permute-start | bytes 1013768 | tf_op jit(solution)/shard_map/ppermute | solution.py:18
  104.2 23.9 %collective-permute-start.9 = (f32[5,22,3,256]{3,1,2,0:T(8,128)}, f32[5,22,3,256]{3,1,2,0:T(8,128)}, u32[]{:S(2)}, u32[]{:S(2)}) collective-permute-start(f32[5,22,3,256]{3,1,2,0:T(8,128)} %copy.56), channel_id=1, source_target_pairs={{4,0},{8,4},{12,8},{5,1},{9,5},{13,9},{6,2},{10,6},{14,10},{7,3},{... | collective-permute-start | bytes 1013768 | tf_op jit(solution)/shard_map/ppermute | solution.py:19
  160.2 19.6 %collective-permute-start.10 = (f32[5,22,22,3]{2,1,3,0:T(8,128)}, f32[5,22,22,3]{2,1,3,0:T(8,128)}, u32[]{:S(2)}, u32[]{:S(2)}) collective-permute-start(f32[5,22,22,3]{2,1,3,0:T(8,128)} %get-tuple-element.28), channel_id=1, source_target_pairs={{0,1},{1,2},{2,3},{4,5},{5,6},{6,7},{8,9},{9,10},{10,11},{12,13},{... | collective-permute-start | bytes 87128 | tf_op jit(solution)/shard_map/ppermute | solution.py:18
  162.9 20.0 %collective-permute-start.11 = (f32[5,22,22,3]{2,1,3,0:T(8,128)}, f32[5,22,22,3]{2,1,3,0:T(8,128)S(1)}, u32[]{:S(2)}, u32[]{:S(2)}) collective-permute-start(f32[5,22,22,3]{2,1,3,0:T(8,128)} %get-tuple-element.29), channel_id=1, source_target_pairs={{1,0},{2,1},{3,2},{5,4},{6,5},{7,6},{9,8},{10,9},{11,10},{13,12},{... | collective-permute-start | bytes 87128 | tf_op jit(solution)/shard_map/ppermute | solution.py:19
  165.1 25.7 %collective-permute-start.4 = (f32[20,20,2]{2,1,0:T(8,128)}, f32[20,20,2]{2,1,0:T(8,128)S(1)}, u32[]{:S(2)}, u32[]{:S(2)}) collective-permute-start(f32[20,20,2]{2,1,0:T(8,128)} %get-tuple-element.38), channel_id=1, source_target_pairs={{0,1},{1,2},{2,3},{4,5},{5,6},{6,7},{8,9},{9,10},{10,11},{12,13},{... | collective-permute-start | bytes 9608 | tf_op jit(solution)/shard_map/ppermute | solution.py:18
  169.1 22.4 %collective-permute-start.5 = (f32[20,20,2]{2,1,0:T(8,128)}, f32[20,20,2]{2,1,0:T(8,128)}, u32[]{:S(2)}, u32[]{:S(2)}) collective-permute-start(f32[20,20,2]{2,1,0:T(8,128)} %get-tuple-element.39), channel_id=1, source_target_pairs={{1,0},{2,1},{3,2},{5,4},{6,5},{7,6},{9,8},{10,9},{11,10},{13,12},{... | collective-permute-start | bytes 9608 | tf_op jit(solution)/shard_map/ppermute | solution.py:19
  204.0 7.3 %collective-permute-start.12 = (f32[1,16,256]{2,1,0:T(8,128)S(1)}, f32[1,16,256]{2,1,0:T(8,128)S(1)}, u32[]{:S(2)}, u32[]{:S(2)}) collective-permute-start(f32[1,16,256]{2,1,0:T(8,128)S(1)} %get-tuple-element.56), channel_id=1, source_target_pairs={{0,16},{16,32},{32,48},{48,64},{64,80},{80,96},{96,112},{1,17},{17... | collective-permute-start | bytes 49160 | tf_op jit(solution)/shard_map/ppermute | solution.py:18
  208.9 5.1 collective-permute-start.13
  214.0 5.6 collective-permute-start.14
  218.3 4.5 collective-permute-start.15
  223.0 9.5 %collective-permute-start.16 = (f32[18,18,1]{2,1,0:T(8,128)S(1)}, f32[18,18,1]{2,1,0:T(8,128)S(1)}, u32[]{:S(2)}, u32[]{:S(2)}) collective-permute-start(f32[18,18,1]{2,1,0:T(8,128)S(1)} %get-tuple-element.42), channel_id=1, source_target_pairs={{0,1},{1,2},{2,3},{4,5},{5,6},{6,7},{8,9},{9,10},{10,11},{12,13},{... | collective-permute-start | bytes 3896 | tf_op jit(solution)/shard_map/ppermute | solution.py:18
  227.2 9.1 %collective-permute-start.17 = (f32[18,18,1]{2,1,0:T(8,128)S(1)}, f32[18,18,1]{2,1,0:T(8,128)S(1)}, u32[]{:S(2)}, u32[]{:S(2)}) collective-permute-start(f32[18,18,1]{2,1,0:T(8,128)S(1)} %get-tuple-element.43), channel_id=1, source_target_pairs={{1,0},{2,1},{3,2},{5,4},{6,5},{7,6},{9,8},{10,9},{11,10},{13,12},{... | collective-permute-start | bytes 3896 | tf_op jit(solution)/shard_map/ppermute | solution.py:19
  353.9 77.2 %collective-permute-start.18 = (f32[2,16,256]{2,1,0:T(8,128)S(1)}, f32[2,16,256]{2,1,0:T(8,128)S(1)}, u32[]{:S(2)}, u32[]{:S(2)}) collective-permute-start(f32[2,16,256]{2,1,0:T(8,128)S(1)} %get-tuple-element.54), channel_id=1, source_target_pairs={{0,16},{16,32},{32,48},{48,64},{64,80},{80,96},{96,112},{1,17},{17... | collective-permute-start | bytes 98312 | tf_op jit(solution)/shard_map/ppermute | solution.py:18
  357.2 73.9 %collective-permute-start.19 = (f32[2,16,256]{2,1,0:T(8,128)S(1)}, f32[2,16,256]{2,1,0:T(8,128)S(1)}, u32[]{:S(2)}, u32[]{:S(2)}) collective-permute-start(f32[2,16,256]{2,1,0:T(8,128)S(1)} %get-tuple-element.55), channel_id=1, source_target_pairs={{16,0},{32,16},{48,32},{64,48},{80,64},{96,80},{112,96},{17,1},{33... | collective-permute-start | bytes 98312 | tf_op jit(solution)/shard_map/ppermute | solution.py:19
  431.1 4.1 collective-permute-start.20
  433.7 4.7 collective-permute-start.21
  438.7 9.8 %collective-permute-start.22 = (f32[20,20,2]{2,1,0:T(8,128)S(1)}, f32[20,20,2]{2,1,0:T(8,128)S(1)}, u32[]{:S(2)}, u32[]{:S(2)}) collective-permute-start(f32[20,20,2]{2,1,0:T(8,128)S(1)} %get-tuple-element.36), channel_id=1, source_target_pairs={{0,1},{1,2},{2,3},{4,5},{5,6},{6,7},{8,9},{9,10},{10,11},{12,13},{... | collective-permute-start | bytes 9608 | tf_op jit(solution)/shard_map/ppermute | solution.py:18
  440.6 7.9 %collective-permute-start.23 = (f32[20,20,2]{2,1,0:T(8,128)S(1)}, f32[20,20,2]{2,1,0:T(8,128)S(1)}, u32[]{:S(2)}, u32[]{:S(2)}) collective-permute-start(f32[20,20,2]{2,1,0:T(8,128)S(1)} %get-tuple-element.37), channel_id=1, source_target_pairs={{1,0},{2,1},{3,2},{5,4},{6,5},{7,6},{9,8},{10,9},{11,10},{13,12},{... | collective-permute-start | bytes 9608 | tf_op jit(solution)/shard_map/ppermute | solution.py:19
  514.5 4.3 collective-permute-start.24
  516.5 5.1 collective-permute-start.25
  521.5 2.7 collective-permute-start.26
  522.9 4.6 collective-permute-start.27
  527.7 6.4 %collective-permute-start.28 = (f32[18,18,1]{2,1,0:T(8,128)S(1)}, f32[18,18,1]{2,1,0:T(8,128)S(1)}, u32[]{:S(2)}, u32[]{:S(2)}) collective-permute-start(f32[18,18,1]{2,1,0:T(8,128)S(1)} %get-tuple-element.40), channel_id=1, source_target_pairs={{0,1},{1,2},{2,3},{4,5},{5,6},{6,7},{8,9},{9,10},{10,11},{12,13},{... | collective-permute-start | bytes 3896 | tf_op jit(solution)/shard_map/ppermute | solution.py:18
  529.0 9.2 %collective-permute-start.29 = (f32[18,18,1]{2,1,0:T(8,128)S(1)}, f32[18,18,1]{2,1,0:T(8,128)S(1)}, u32[]{:S(2)}, u32[]{:S(2)}) collective-permute-start(f32[18,18,1]{2,1,0:T(8,128)S(1)} %get-tuple-element.41), channel_id=1, source_target_pairs={{1,0},{2,1},{3,2},{5,4},{6,5},{7,6},{9,8},{10,9},{11,10},{13,12},{... | collective-permute-start | bytes 3896 | tf_op jit(solution)/shard_map/ppermute | solution.py:19
  (30 other events, 928.1 us)
